TPU v7x, 32 devices: a whole 2x2x4 slice. The times are simulated.
32 devices in a mesh: runs: 2 (over x), gx: 16 (over z, y, core).
Axes of the slice: x: 2, y: 2, z: 4, core: 2. Of those that a mesh axis runs over, the one named last changes fastest.
Arguments:
- potential: float32 [64, 512, 512], P(('runs', 'gx')), parts along dimension 0, may hold values from -3 to 3
Outputs:
- second_potential: float32 [64, 512, 512], P(('runs', 'gx')), parts along dimension 0
- norms: float32 [4], P('runs'), parts along dimension 0
There are 2 independent parts, one for each index of `runs`. A program takes and returns all parts, laid end to end along the dimension named above; each array names one. Nothing has to cross between parts.
All inputs are finite; a program needn't handle non-finite values.
Results may differ from a plain program's by a relative error of at most 0.00015.
Values sent between devices are 32-bit elements; how exact they have to be, the bound alone decides.
A program may use at most 256 MiB of HBM per device.

v0:
```python
import jax
import jax.numpy as jnp
from jax import lax
from jax.sharding import PartitionSpec as P

LEVELS = 2
COARSE = 4
CYCLES = 2


RELAX = 0.8


def with_halo(cells, sides, width):
    for axis, dim in sides:
        count = lax.axis_size(axis)
        head = lax.slice_in_dim(cells, 0, width, axis=dim)
        tail = lax.slice_in_dim(cells, cells.shape[dim] - width, cells.shape[dim], axis=dim)
        cells = jnp.concatenate(
            [
                lax.ppermute(tail, axis, [(i, (i + 1) % count) for i in range(count)]),
                cells,
                lax.ppermute(head, axis, [((i + 1) % count, i) for i in range(count)]),
            ],
            axis=dim,
        )
    return cells


def shifted(field, offset, axis):
    return jnp.roll(field, -offset, axis)


def source_term(padded):
    center = padded[1:-1]
    upper = padded[2:]
    lower = padded[:-2]
    curve_xx = upper + lower - 2.0 * center
    curve_yy = shifted(center, 1, 1) + shifted(center, -1, 1) - 2.0 * center
    curve_zz = shifted(center, 1, 2) + shifted(center, -1, 2) - 2.0 * center
    cross_xy = (
        shifted(upper, 1, 1) - shifted(upper, -1, 1) - shifted(lower, 1, 1) + shifted(lower, -1, 1)
    ) * 0.25
    cross_xz = (
        shifted(upper, 1, 2) - shifted(upper, -1, 2) - shifted(lower, 1, 2) + shifted(lower, -1, 2)
    ) * 0.25
    plus_y = shifted(center, 1, 1)
    minus_y = shifted(center, -1, 1)
    cross_yz = (
        shifted(plus_y, 1, 2)
        - shifted(plus_y, -1, 2)
        - shifted(minus_y, 1, 2)
        + shifted(minus_y, -1, 2)
    ) * 0.25
    return (
        curve_xx * curve_yy
        - cross_xy * cross_xy
        + curve_xx * curve_zz
        - cross_xz * cross_xz
        + curve_yy * curve_zz
        - cross_yz * cross_yz
    )


def operator(padded, spacing):
    center = padded[1:-1]
    beside_all = padded[2:] + padded[:-2]
    beside_all = beside_all + shifted(center, 1, 1) + shifted(center, -1, 1)
    beside_all = beside_all + shifted(center, 1, 2) + shifted(center, -1, 2)
    return (6.0 * center - beside_all) / spacing


def relax(padded, forcing, spacing):
    return padded[1:-1] + RELAX * spacing / 6.0 * (forcing - operator(padded, spacing))


def restrict(field):
    planes, rows, cols = field.shape
    blocks = field.reshape(planes // 2, 2, rows // 2, 2, cols // 2, 2)
    return jnp.mean(blocks, axis=(1, 3, 5))


def prolong(field):
    return jnp.repeat(jnp.repeat(jnp.repeat(field, 2, 0), 2, 1), 2, 2)


def smooth(field, forcing, spacing):
    padded = with_halo(field, (("gx", 0),), 1)
    field = relax(padded, forcing, spacing)
    return field


def residual_of(field, forcing, spacing):
    padded = with_halo(field, (("gx", 0),), 1)
    return forcing - operator(padded, spacing)


def report_norm(residue, cell_count):
    squares = lax.psum(jnp.sum(residue * residue), "gx")
    return jnp.sqrt(squares / cell_count)


def coarsest_solve(forcing, spacing):
    field = jnp.zeros_like(forcing)
    for sweep_index in range(COARSE):
        padded = with_halo(field, (("gx", 0),), 1)
        field = relax(padded, forcing, spacing)
    return field


def vcycle(field, forcing, level):
    spacing = float(4**level)
    if level == LEVELS - 1:
        return coarsest_solve(forcing, spacing)
    field = smooth(field, forcing, spacing)
    residue = residual_of(field, forcing, spacing)
    coarse_rhs = restrict(residue)
    correction = vcycle(jnp.zeros_like(coarse_rhs), coarse_rhs, level + 1)
    field = field + prolong(correction)
    return smooth(field, forcing, spacing)


def on_device(potential):
    devices_x = lax.axis_size("gx")
    padded = with_halo(potential, (("gx", 0),), 1)
    source = source_term(padded)
    cell_count = float(source.size * devices_x)
    total = lax.psum(jnp.sum(source), "gx")
    forcing = -(source - total / cell_count)
    field = jnp.zeros_like(forcing)
    results = []
    for cycle_index in range(CYCLES):
        field = vcycle(field, forcing, 0)
        residue = residual_of(field, forcing, 1.0)
        results.append(report_norm(residue, cell_count))
    return (field, jnp.stack(results))


def solution(mesh):
    in_specs = (P(("runs", "gx"), None, None),)
    out_specs = (P(("runs", "gx"), None, None), P("runs"))
    return jax.shard_map(
        on_device, mesh=mesh, in_specs=in_specs, out_specs=out_specs, check_vma=False
    )
```

profile of v0, /device:TPU:0, one launch (start us, length us, event | category | flops | bytes accessed | tf_op | source)
XLA Modules:
  0.0 568.8 jit_solution(14967291704961205663)
XLA Ops:
  1.7 5.5 collective-permute-start.2
  9.0 4.5 collective-permute-start
  19.3 16.4 %collective-permute-done.1 = f32[1,512,512]{2,1,0:T(8,128)S(1)} collective-permute-done((f32[1,512,512]{2,1,0:T(8,128)S(1)}, f32[1,512,512]{2,1,0:T(8,128)S(1)}, u32[]{:S(2)}, u32[]{:S(2)}) %collective-permute-start.1) | collective-permute-done | bytes 1048608 | tf_op jit(solution)/shard_map/ppermute | solution.py:21
  35.7 17.6 %collective-permute-start.7 = (f32[1,256,256]{2,1,0:T(8,128)}, f32[1,256,256]{2,1,0:T(8,128)}, u32[]{:S(2)}, u32[]{:S(2)}) collective-permute-start(f32[1,256,256]{2,1,0:T(8,128)} %broadcast.125), channel_id=1, source_target_pairs={{0,1},{1,2},{2,3},{3,4},{4,5},{5,6},{6,7},{7,8},{8,9},{9,10},{10,1... | collective-permute-start | bytes 786440 | tf_op jit(solution)/shard_map/ppermute | solution.py:21
  55.8 2.7 fusion.144
  59.7 2.4 fusion.142
  62.1 2.7 fusion.146
  66.0 10.8 %fusion.138 = (f32[]{:T(128)}, f32[2,512,512]{2,1,0:T(8,128)S(1)}) fusion(f32[2,512,511]{2,1,0:T(8,128)S(1)} %get-tuple-element.33, f32[2,512,1]{2,1,0:T(8,128)S(1)} %get-tuple-element.35, f32[2,512,1]{2,1,0:T(8,128)S(1)} %get-tuple-element.34, f32[2,512,511]{2,1,0:T(8,128)S(1)} %get-tuple-element.32, f32[2,512,511]{2,1,0:T(8,128)S(1)} %get-tuple-element.156, ...), kind=kLoop, calls=%fused_computation.189 | loop fusion | flops 24641536 | bytes 41943044 | tf_op jit(solution)/shard_map/reduce_sum | solution.py:128
  76.8 32.6 %psum.21 = f32[]{:T(128)} all-reduce(f32[]{:T(128)} %get-tuple-element.10), channel_id=1, replica_groups=mesh['runs'=2,'gx'=16] {'gx'}, use_global_device_ids=true, to_apply=%region_1.2 | all-reduce | flops 1 | bytes 8 | tf_op jit(solution)/shard_map/psum | solution.py:128
  110.1 2.1 broadcast_multiply_fusion
  114.5 10.2 %collective-permute-done.4 = f32[1,512,512]{2,1,0:T(8,128)S(1)} collective-permute-done((f32[1,512,512]{2,1,0:T(8,128)S(1)}, f32[1,512,512]{2,1,0:T(8,128)S(1)}, u32[]{:S(2)}, u32[]{:S(2)}) %collective-permute-start.4) | collective-permute-done | bytes 1048608 | tf_op jit(solution)/shard_map/ppermute | solution.py:23
  124.7 4.9 collective-permute-done.5
  129.6 2.7 fusion.59
  132.3 68.4 %reduce_sum.61 = f32[256,2,256,2]{3,2,1,0:T(8,128)} reshape(f32[512,512]{1,0:T(8,128)S(1)} %fusion.59) | data formatting | bytes 2097152 | tf_op jit(solution)/shard_map/reduce_sum | solution.py:80
  200.7 21.0 %reduce_sum.62 = f32[256,256]{1,0:T(8,128)S(1)} reduce(f32[256,2,256,2]{3,2,1,0:T(8,128)} %reduce_sum.61, f32[]{:T(128)} %constant.41.clone.1), dimensions={1,3}, to_apply=%region_3.4 | reduce | flops 196608 | bytes 1310724 | tf_op jit(solution)/shard_map/reduce_sum | solution.py:80
  223.8 6.7 %collective-permute-start.9 = (f32[1,256,256]{2,1,0:T(8,128)S(1)}, f32[1,256,256]{2,1,0:T(8,128)S(1)}, u32[]{:S(2)}, u32[]{:S(2)}) collective-permute-start(f32[1,256,256]{2,1,0:T(8,128)S(1)} %get-tuple-element.6), channel_id=1, source_target_pairs={{0,1},{1,2},{2,3},{3,4},{4,5},{5,6},{6,7},{7,8},{8,9},{9,10},{10,1... | collective-permute-start | bytes 786440 | tf_op jit(solution)/shard_map/ppermute | solution.py:21
  231.4 2.9 collective-permute-done.9
  234.7 2.6 collective-permute-start.11
  238.6 4.8 collective-permute-done.11
  243.8 2.6 collective-permute-start.13
  247.7 4.8 collective-permute-done.13
  261.1 2.5 collective-permute-start.15
  265.1 8.3 %collective-permute-done.14 = f32[1,512,512]{2,1,0:T(8,128)S(1)} collective-permute-done((f32[1,512,512]{2,1,0:T(8,128)S(1)}, f32[1,512,512]{2,1,0:T(8,128)S(1)}, u32[]{:S(2)}, u32[]{:S(2)}) %collective-permute-start.14) | collective-permute-done | bytes 1048608 | tf_op jit(solution)/shard_map/ppermute | solution.py:23
  273.4 4.8 collective-permute-done.15
  278.2 2.6 fusion.51
  281.2 16.5 %collective-permute-start.17 = (f32[1,512,512]{2,1,0:T(8,128)S(1)}, f32[1,512,512]{2,1,0:T(8,128)S(1)}, u32[]{:S(2)}, u32[]{:S(2)}) collective-permute-start(f32[1,512,512]{2,1,0:T(8,128)S(1)} %get-tuple-element.67), channel_id=1, source_target_pairs={{0,1},{1,2},{2,3},{3,4},{4,5},{5,6},{6,7},{7,8},{8,9},{9,10},{10,1... | collective-permute-start | bytes 3145736 | tf_op jit(solution)/shard_map/ppermute | solution.py:21
  299.8 16.0 %collective-permute-done.17 = f32[1,512,512]{2,1,0:T(8,128)S(1)} collective-permute-done((f32[1,512,512]{2,1,0:T(8,128)S(1)}, f32[1,512,512]{2,1,0:T(8,128)S(1)}, u32[]{:S(2)}, u32[]{:S(2)}) %collective-permute-start.17) | collective-permute-done | bytes 1048608 | tf_op jit(solution)/shard_map/ppermute | solution.py:21
  315.9 3.1 multiply_reduce_fusion
  319.7 8.1 %collective-permute-start.19 = (f32[1,512,512]{2,1,0:T(8,128)S(1)}, f32[1,512,512]{2,1,0:T(8,128)S(1)}, u32[]{:S(2)}, u32[]{:S(2)}) collective-permute-start(f32[1,512,512]{2,1,0:T(8,128)S(1)} %get-tuple-element.65), channel_id=1, source_target_pairs={{0,1},{1,2},{2,3},{3,4},{4,5},{5,6},{6,7},{7,8},{8,9},{9,10},{10,1... | collective-permute-start | bytes 3145736 | tf_op jit(solution)/shard_map/ppermute | solution.py:21
  329.2 2.8 collective-permute-done.18
  332.0 5.3 collective-permute-done.19
  337.3 2.6 fusion.35
  340.0 68.4 %reduce_sum.64 = f32[256,2,256,2]{3,2,1,0:T(8,128)} reshape(f32[512,512]{1,0:T(8,128)S(1)} %fusion.35) | data formatting | bytes 2097152 | tf_op jit(solution)/shard_map/reduce_sum | solution.py:80
  408.3 21.0 %reduce_sum.65 = f32[256,256]{1,0:T(8,128)S(1)} reduce(f32[256,2,256,2]{3,2,1,0:T(8,128)} %reduce_sum.64, f32[]{:T(128)} %constant.41.clone.1), dimensions={1,3}, to_apply=%region_5.6 | reduce | flops 196608 | bytes 1310724 | tf_op jit(solution)/shard_map/reduce_sum | solution.py:80
  429.6 11.0 %collective-permute-start.21 = (f32[1,256,256]{2,1,0:T(8,128)S(1)}, f32[1,256,256]{2,1,0:T(8,128)S(1)}, u32[]{:S(2)}, u32[]{:S(2)}) collective-permute-start(f32[1,256,256]{2,1,0:T(8,128)S(1)} %fusion.134), channel_id=1, source_target_pairs={{0,1},{1,2},{2,3},{3,4},{4,5},{5,6},{6,7},{7,8},{8,9},{9,10},{10,1... | collective-permute-start | bytes 786440 | tf_op jit(solution)/shard_map/ppermute | solution.py:21
  441.6 3.4 collective-permute-done.21
  445.4 2.6 collective-permute-start.23
  449.3 4.8 collective-permute-done.23
  454.5 2.8 collective-permute-start.25
  458.4 5.0 collective-permute-done.25
  470.4 2.2 collective-permute-start.27
  474.1 8.6 %collective-permute-done.26 = f32[1,512,512]{2,1,0:T(8,128)S(1)} collective-permute-done((f32[1,512,512]{2,1,0:T(8,128)S(1)}, f32[1,512,512]{2,1,0:T(8,128)S(1)}, u32[]{:S(2)}, u32[]{:S(2)}) %collective-permute-start.26) | collective-permute-done | bytes 1048608 | tf_op jit(solution)/shard_map/ppermute | solution.py:23
  482.7 4.8 collective-permute-done.27
  487.5 2.6 fusion.27
  490.4 16.6 %collective-permute-start.29 = (f32[1,512,512]{2,1,0:T(8,128)S(1)}, f32[1,512,512]{2,1,0:T(8,128)S(1)}, u32[]{:S(2)}, u32[]{:S(2)}) collective-permute-start(f32[1,512,512]{2,1,0:T(8,128)S(1)} %get-tuple-element.37), channel_id=1, source_target_pairs={{0,1},{1,2},{2,3},{3,4},{4,5},{5,6},{6,7},{7,8},{8,9},{9,10},{10,1... | collective-permute-start | bytes 3145736 | tf_op jit(solution)/shard_map/ppermute | solution.py:21
  509.0 16.9 %collective-permute-done.29 = f32[1,512,512]{2,1,0:T(8,128)S(1)} collective-permute-done((f32[1,512,512]{2,1,0:T(8,128)S(1)}, f32[1,512,512]{2,1,0:T(8,128)S(1)}, u32[]{:S(2)}, u32[]{:S(2)}) %collective-permute-start.29) | collective-permute-done | bytes 1048608 | tf_op jit(solution)/shard_map/ppermute | solution.py:21
  525.9 3.2 fusion.79
  529.1 37.3 %all-reduce.4 = (f32[]{:T(128)}, f32[]{:T(128)}) all-reduce(f32[]{:T(128)} %fusion.79, f32[]{:T(128)} %get-tuple-element.4), channel_id=1, replica_groups=mesh['runs'=2,'gx'=16] {'gx'}, use_global_device_ids=true, to_apply=%region_9.10 | all-reduce | flops 2 | bytes 16 | tf_op jit(solution)/shard_map/psum | solution.py:99
  (142 shorter events, 52.4 us)
Async XLA Ops:
  1.7 12.9 %copy-start.3 = (f32[2,512,512]{2,1,0:T(8,128)S(1)}, f32[2,512,512]{2,1,0:T(8,128)}, u32[]{:S(2)}) copy-start(f32[2,512,512]{2,1,0:T(8,128)} %param.1) | copy-start | bytes 6291460
  1.7 108.3 %collective-permute-start.2 = (f32[1,512,512]{2,1,0:T(8,128)}, f32[1,512,512]{2,1,0:T(8,128)}, u32[]{:S(2)}, u32[]{:S(2)}) collective-permute-start(f32[1,512,512]{2,1,0:T(8,128)} %broadcast.122), channel_id=1, source_target_pairs={{1,0},{2,1},{3,2},{4,3},{5,4},{6,5},{7,6},{8,7},{9,8},{10,9},{11,1... | collective-permute-start | bytes 3145736 | tf_op jit(solution)/shard_map/ppermute | solution.py:23
  7.2 102.8 %collective-permute-start.3 = (f32[1,512,512]{2,1,0:T(8,128)}, f32[1,512,512]{2,1,0:T(8,128)}, u32[]{:S(2)}, u32[]{:S(2)}) collective-permute-start(f32[1,512,512]{2,1,0:T(8,128)} %broadcast.122), channel_id=1, source_target_pairs={{0,1},{1,2},{2,3},{3,4},{4,5},{5,6},{6,7},{7,8},{8,9},{9,10},{10,1... | collective-permute-start | bytes 3145736 | tf_op jit(solution)/shard_map/ppermute | solution.py:21
  8.9 26.8 %collective-permute-start.1 = (f32[1,512,512]{2,1,0:T(8,128)S(1)}, f32[1,512,512]{2,1,0:T(8,128)S(1)}, u32[]{:S(2)}, u32[]{:S(2)}) collective-permute-start(f32[1,512,512]{2,1,0:T(8,128)S(1)} %get-tuple-element.101), channel_id=1, source_target_pairs={{0,1},{1,2},{2,3},{3,4},{4,5},{5,6},{6,7},{7,8},{8,9},{9,10},{10,1... | collective-permute-start | bytes 3145736 | tf_op jit(solution)/shard_map/ppermute | solution.py:21
  9.0 45.0 %collective-permute-start = (f32[1,512,512]{2,1,0:T(8,128)S(1)}, f32[1,512,512]{2,1,0:T(8,128)S(1)}, u32[]{:S(2)}, u32[]{:S(2)}) collective-permute-start(f32[1,512,512]{2,1,0:T(8,128)S(1)} %get-tuple-element.100), channel_id=1, source_target_pairs={{1,0},{2,1},{3,2},{4,3},{5,4},{6,5},{7,6},{8,7},{9,8},{10,9},{11,1... | collective-permute-start | bytes 3145736 | tf_op jit(solution)/shard_map/ppermute | solution.py:23
  14.2 207.5 %collective-permute-start.6 = (f32[1,256,256]{2,1,0:T(8,128)}, f32[1,256,256]{2,1,0:T(8,128)S(1)}, u32[]{:S(2)}, u32[]{:S(2)}) collective-permute-start(f32[1,256,256]{2,1,0:T(8,128)} %broadcast.125), channel_id=1, source_target_pairs={{1,0},{2,1},{3,2},{4,3},{5,4},{6,5},{7,6},{8,7},{9,8},{10,9},{11,1... | collective-permute-start | bytes 786440 | tf_op jit(solution)/shard_map/ppermute | solution.py:23
  35.7 186.7 %collective-permute-start.7 = (f32[1,256,256]{2,1,0:T(8,128)}, f32[1,256,256]{2,1,0:T(8,128)}, u32[]{:S(2)}, u32[]{:S(2)}) collective-permute-start(f32[1,256,256]{2,1,0:T(8,128)} %broadcast.125), channel_id=1, source_target_pairs={{0,1},{1,2},{2,3},{3,4},{4,5},{5,6},{6,7},{7,8},{8,9},{9,10},{10,1... | collective-permute-start | bytes 786440 | tf_op jit(solution)/shard_map/ppermute | solution.py:21
  76.8 239.1 %copy-start = (f32[2,512,512]{2,1,0:T(8,128)}, f32[2,512,512]{2,1,0:T(8,128)S(1)}, u32[]{:S(2)}) copy-start(f32[2,512,512]{2,1,0:T(8,128)S(1)} %get-tuple-element.11) | copy-start | bytes 6291460
  112.1 17.5 %copy-start.5 = (f32[2,512,512]{2,1,0:T(8,128)}, f32[2,512,512]{2,1,0:T(8,128)S(1)}, u32[]{:S(2)}) copy-start(f32[2,512,512]{2,1,0:T(8,128)S(1)} %get-tuple-element.9) | copy-start | bytes 6291460
  112.3 12.4 %collective-permute-start.4 = (f32[1,512,512]{2,1,0:T(8,128)S(1)}, f32[1,512,512]{2,1,0:T(8,128)S(1)}, u32[]{:S(2)}, u32[]{:S(2)}) collective-permute-start(f32[1,512,512]{2,1,0:T(8,128)S(1)} %get-tuple-element.94), channel_id=1, source_target_pairs={{1,0},{2,1},{3,2},{4,3},{5,4},{6,5},{7,6},{8,7},{9,8},{10,9},{11,1... | collective-permute-start | bytes 3145736 | tf_op jit(solution)/shard_map/ppermute | solution.py:23
  112.4 17.2 %collective-permute-start.5 = (f32[1,512,512]{2,1,0:T(8,128)S(1)}, f32[1,512,512]{2,1,0:T(8,128)S(1)}, u32[]{:S(2)}, u32[]{:S(2)}) collective-permute-start(f32[1,512,512]{2,1,0:T(8,128)S(1)} %get-tuple-element.95), channel_id=1, source_target_pairs={{0,1},{1,2},{2,3},{3,4},{4,5},{5,6},{6,7},{7,8},{8,9},{9,10},{10,1... | collective-permute-start | bytes 3145736 | tf_op jit(solution)/shard_map/ppermute | solution.py:21
  221.7 0.7 copy-start.6
  223.7 7.7 %collective-permute-start.8 = (f32[1,256,256]{2,1,0:T(8,128)S(1)}, f32[1,256,256]{2,1,0:T(8,128)S(1)}, u32[]{:S(2)}, u32[]{:S(2)}) collective-permute-start(f32[1,256,256]{2,1,0:T(8,128)S(1)} %get-tuple-element.6), channel_id=1, source_target_pairs={{1,0},{2,1},{3,2},{4,3},{5,4},{6,5},{7,6},{8,7},{9,8},{10,9},{11,1... | collective-permute-start | bytes 786440 | tf_op jit(solution)/shard_map/ppermute | solution.py:23
  223.8 10.5 %collective-permute-start.9 = (f32[1,256,256]{2,1,0:T(8,128)S(1)}, f32[1,256,256]{2,1,0:T(8,128)S(1)}, u32[]{:S(2)}, u32[]{:S(2)}) collective-permute-start(f32[1,256,256]{2,1,0:T(8,128)S(1)} %get-tuple-element.6), channel_id=1, source_target_pairs={{0,1},{1,2},{2,3},{3,4},{4,5},{5,6},{6,7},{7,8},{8,9},{9,10},{10,1... | collective-permute-start | bytes 786440 | tf_op jit(solution)/shard_map/ppermute | solution.py:21
  234.7 3.9 collective-permute-start.10
  234.7 8.6 %collective-permute-start.11 = (f32[1,256,256]{2,1,0:T(8,128)S(1)}, f32[1,256,256]{2,1,0:T(8,128)S(1)}, u32[]{:S(2)}, u32[]{:S(2)}) collective-permute-start(f32[1,256,256]{2,1,0:T(8,128)S(1)} %fusion.91), channel_id=1, source_target_pairs={{0,1},{1,2},{2,3},{3,4},{4,5},{5,6},{6,7},{7,8},{8,9},{9,10},{10,1... | collective-permute-start | bytes 786440 | tf_op jit(solution)/shard_map/ppermute | solution.py:21
  243.7 3.9 collective-permute-start.12
  243.8 8.6 %collective-permute-start.13 = (f32[1,256,256]{2,1,0:T(8,128)S(1)}, f32[1,256,256]{2,1,0:T(8,128)S(1)}, u32[]{:S(2)}, u32[]{:S(2)}) collective-permute-start(f32[1,256,256]{2,1,0:T(8,128)S(1)} %fusion.99), channel_id=1, source_target_pairs={{0,1},{1,2},{2,3},{3,4},{4,5},{5,6},{6,7},{7,8},{8,9},{9,10},{10,1... | collective-permute-start | bytes 786440 | tf_op jit(solution)/shard_map/ppermute | solution.py:21
  261.0 12.4 %collective-permute-start.14 = (f32[1,512,512]{2,1,0:T(8,128)S(1)}, f32[1,512,512]{2,1,0:T(8,128)S(1)}, u32[]{:S(2)}, u32[]{:S(2)}) collective-permute-start(f32[1,512,512]{2,1,0:T(8,128)S(1)} %get-tuple-element.84), channel_id=1, source_target_pairs={{1,0},{2,1},{3,2},{4,3},{5,4},{6,5},{7,6},{8,7},{9,8},{10,9},{11,1... | collective-permute-start | bytes 3145736 | tf_op jit(solution)/shard_map/ppermute | solution.py:23
  261.1 17.1 %collective-permute-start.15 = (f32[1,512,512]{2,1,0:T(8,128)S(1)}, f32[1,512,512]{2,1,0:T(8,128)S(1)}, u32[]{:S(2)}, u32[]{:S(2)}) collective-permute-start(f32[1,512,512]{2,1,0:T(8,128)S(1)} %get-tuple-element.85), channel_id=1, source_target_pairs={{0,1},{1,2},{2,3},{3,4},{4,5},{5,6},{6,7},{7,8},{8,9},{9,10},{10,1... | collective-permute-start | bytes 3145736 | tf_op jit(solution)/shard_map/ppermute | solution.py:21
  280.9 18.9 %collective-permute-start.16 = (f32[1,512,512]{2,1,0:T(8,128)S(1)}, f32[1,512,512]{2,1,0:T(8,128)S(1)}, u32[]{:S(2)}, u32[]{:S(2)}) collective-permute-start(f32[1,512,512]{2,1,0:T(8,128)S(1)} %get-tuple-element.66), channel_id=1, source_target_pairs={{1,0},{2,1},{3,2},{4,3},{5,4},{6,5},{7,6},{8,7},{9,8},{10,9},{11,1... | collective-permute-start | bytes 3145736 | tf_op jit(solution)/shard_map/ppermute | solution.py:23
  281.2 34.7 %collective-permute-start.17 = (f32[1,512,512]{2,1,0:T(8,128)S(1)}, f32[1,512,512]{2,1,0:T(8,128)S(1)}, u32[]{:S(2)}, u32[]{:S(2)}) collective-permute-start(f32[1,512,512]{2,1,0:T(8,128)S(1)} %get-tuple-element.67), channel_id=1, source_target_pairs={{0,1},{1,2},{2,3},{3,4},{4,5},{5,6},{6,7},{7,8},{8,9},{9,10},{10,1... | collective-permute-start | bytes 3145736 | tf_op jit(solution)/shard_map/ppermute | solution.py:21
  319.7 12.4 %collective-permute-start.18 = (f32[1,512,512]{2,1,0:T(8,128)S(1)}, f32[1,512,512]{2,1,0:T(8,128)S(1)}, u32[]{:S(2)}, u32[]{:S(2)}) collective-permute-start(f32[1,512,512]{2,1,0:T(8,128)S(1)} %get-tuple-element.64), channel_id=1, source_target_pairs={{1,0},{2,1},{3,2},{4,3},{5,4},{6,5},{7,6},{8,7},{9,8},{10,9},{11,1... | collective-permute-start | bytes 3145736 | tf_op jit(solution)/shard_map/ppermute | solution.py:23
  319.7 17.6 %collective-permute-start.19 = (f32[1,512,512]{2,1,0:T(8,128)S(1)}, f32[1,512,512]{2,1,0:T(8,128)S(1)}, u32[]{:S(2)}, u32[]{:S(2)}) collective-permute-start(f32[1,512,512]{2,1,0:T(8,128)S(1)} %get-tuple-element.65), channel_id=1, source_target_pairs={{0,1},{1,2},{2,3},{3,4},{4,5},{5,6},{6,7},{7,8},{8,9},{9,10},{10,1... | collective-permute-start | bytes 3145736 | tf_op jit(solution)/shard_map/ppermute | solution.py:21
  328.7 8.6 %copy-start.1 = (f32[2,512,512]{2,1,0:T(8,128)S(1)}, f32[2,512,512]{2,1,0:T(8,128)}, u32[]{:S(2)}) copy-start(f32[2,512,512]{2,1,0:T(8,128)} %copy-done) | copy-start | bytes 6291460
  429.5 12.0 %collective-permute-start.20 = (f32[1,256,256]{2,1,0:T(8,128)S(1)}, f32[1,256,256]{2,1,0:T(8,128)S(1)}, u32[]{:S(2)}, u32[]{:S(2)}) collective-permute-start(f32[1,256,256]{2,1,0:T(8,128)S(1)} %fusion.134), channel_id=1, source_target_pairs={{1,0},{2,1},{3,2},{4,3},{5,4},{6,5},{7,6},{8,7},{9,8},{10,9},{11,1... | collective-permute-start | bytes 786440 | tf_op jit(solution)/shard_map/ppermute | solution.py:23
  429.6 15.4 %collective-permute-start.21 = (f32[1,256,256]{2,1,0:T(8,128)S(1)}, f32[1,256,256]{2,1,0:T(8,128)S(1)}, u32[]{:S(2)}, u32[]{:S(2)}) collective-permute-start(f32[1,256,256]{2,1,0:T(8,128)S(1)} %fusion.134), channel_id=1, source_target_pairs={{0,1},{1,2},{2,3},{3,4},{4,5},{5,6},{6,7},{7,8},{8,9},{9,10},{10,1... | collective-permute-start | bytes 786440 | tf_op jit(solution)/shard_map/ppermute | solution.py:21
  445.4 3.9 collective-permute-start.22
  445.4 8.6 %collective-permute-start.23 = (f32[1,256,256]{2,1,0:T(8,128)S(1)}, f32[1,256,256]{2,1,0:T(8,128)S(1)}, u32[]{:S(2)}, u32[]{:S(2)}) collective-permute-start(f32[1,256,256]{2,1,0:T(8,128)S(1)} %fusion.116), channel_id=1, source_target_pairs={{0,1},{1,2},{2,3},{3,4},{4,5},{5,6},{6,7},{7,8},{8,9},{9,10},{10,1... | collective-permute-start | bytes 786440 | tf_op jit(solution)/shard_map/ppermute | solution.py:21
  454.4 3.9 collective-permute-start.24
  454.5 8.9 %collective-permute-start.25 = (f32[1,256,256]{2,1,0:T(8,128)S(1)}, f32[1,256,256]{2,1,0:T(8,128)S(1)}, u32[]{:S(2)}, u32[]{:S(2)}) collective-permute-start(f32[1,256,256]{2,1,0:T(8,128)S(1)} %fusion.124), channel_id=1, source_target_pairs={{0,1},{1,2},{2,3},{3,4},{4,5},{5,6},{6,7},{7,8},{8,9},{9,10},{10,1... | collective-permute-start | bytes 786440 | tf_op jit(solution)/shard_map/ppermute | solution.py:21
  470.4 12.4 %collective-permute-start.26 = (f32[1,512,512]{2,1,0:T(8,128)S(1)}, f32[1,512,512]{2,1,0:T(8,128)S(1)}, u32[]{:S(2)}, u32[]{:S(2)}) collective-permute-start(f32[1,512,512]{2,1,0:T(8,128)S(1)} %get-tuple-element.54), channel_id=1, source_target_pairs={{1,0},{2,1},{3,2},{4,3},{5,4},{6,5},{7,6},{8,7},{9,8},{10,9},{11,1... | collective-permute-start | bytes 3145736 | tf_op jit(solution)/shard_map/ppermute | solution.py:23
  470.4 17.1 %collective-permute-start.27 = (f32[1,512,512]{2,1,0:T(8,128)S(1)}, f32[1,512,512]{2,1,0:T(8,128)S(1)}, u32[]{:S(2)}, u32[]{:S(2)}) collective-permute-start(f32[1,512,512]{2,1,0:T(8,128)S(1)} %get-tuple-element.55), channel_id=1, source_target_pairs={{0,1},{1,2},{2,3},{3,4},{4,5},{5,6},{6,7},{7,8},{8,9},{9,10},{10,1... | collective-permute-start | bytes 3145736 | tf_op jit(solution)/shard_map/ppermute | solution.py:21
  473.6 13.9 %copy-start.2 = (f32[2,512,512]{2,1,0:T(8,128)S(1)}, f32[2,512,512]{2,1,0:T(8,128)}, u32[]{:S(2)}) copy-start(f32[2,512,512]{2,1,0:T(8,128)} %copy-done) | copy-start | bytes 6291460
  490.1 35.8 %copy-start.4 = (f32[2,512,512]{2,1,0:T(8,128)}, f32[2,512,512]{2,1,0:T(8,128)S(1)}, u32[]{:S(2)}) copy-start(f32[2,512,512]{2,1,0:T(8,128)S(1)} %fusion.27) | copy-start | bytes 6291460
  490.3 18.7 %collective-permute-start.28 = (f32[1,512,512]{2,1,0:T(8,128)S(1)}, f32[1,512,512]{2,1,0:T(8,128)S(1)}, u32[]{:S(2)}, u32[]{:S(2)}) collective-permute-start(f32[1,512,512]{2,1,0:T(8,128)S(1)} %get-tuple-element.36), channel_id=1, source_target_pairs={{1,0},{2,1},{3,2},{4,3},{5,4},{6,5},{7,6},{8,7},{9,8},{10,9},{11,1... | collective-permute-start | bytes 3145736 | tf_op jit(solution)/shard_map/ppermute | solution.py:23
  490.4 35.6 %collective-permute-start.29 = (f32[1,512,512]{2,1,0:T(8,128)S(1)}, f32[1,512,512]{2,1,0:T(8,128)S(1)}, u32[]{:S(2)}, u32[]{:S(2)}) collective-permute-start(f32[1,512,512]{2,1,0:T(8,128)S(1)} %get-tuple-element.37), channel_id=1, source_target_pairs={{0,1},{1,2},{2,3},{3,4},{4,5},{5,6},{6,7},{7,8},{8,9},{9,10},{10,1... | collective-permute-start | bytes 3145736 | tf_op jit(solution)/shard_map/ppermute | solution.py:21
where the time goes:
time: 576 us; the launch traced here: 569 us
  local copies, waits for them, and re-layouts  180 us (31%)
  waiting for transfers between devices  132 us (23%)
  starting transfers between devices  104 us (18%)
  other arithmetic  79.7 us (14%)
  blocking collectives  69.9 us (12%)
    reduce_sum x2, local copies, waits for them, and re-layouts, restrict(): return jnp.mean(blocks, axis=(1, 3, 5))  137 us
    ppermute x15, waiting for transfers between devices, with_halo(): lax.ppermute(tail, axis, [(i, (i + 1) % count) for i in range(count)])  94.7 us
    ppermute x15, starting transfers between devices, with_halo(): lax.ppermute(tail, axis, [(i, (i + 1) % count) for i in range(count)])  92.5 us
    reduce_sum x4, other arithmetic, restrict(): return jnp.mean(blocks, axis=(1, 3, 5))  47.4 us
    psum x1, blocking collectives, report_norm(): squares = lax.psum(jnp.sum(residue * residue), 'gx')  37.3 us
    ppermute x15, waiting for transfers between devices, with_halo(): lax.ppermute(head, axis, [((i + 1) % count, i) for i in range(count)])  37.3 us
    psum x1, blocking collectives, on_device(): total = lax.psum(jnp.sum(source), 'gx')  32.6 us
    slice x62, local copies, waits for them, and re-layouts, shifted(): return jnp.roll(field, -offset, axis)  24.4 us
  transfers between devices with their start and end apart: 30, of which 25 were waited for; matrix products, arithmetic and copies ran while one was open for 24% of the time, Pallas kernels for 0%

commit v1 on v0

v1 whole, which is shorter than its diff:
```python
import functools

import jax
import jax.numpy as jnp
from jax import lax
from jax.experimental import pallas as pl
from jax.experimental.pallas import tpu as pltpu
from jax.sharding import PartitionSpec as P

GROUP = 4
HX = 5
HY = 24
PAD = 8
CH = 16
A = 0.8 / 6.0
F32 = jnp.float32
BF16 = jnp.bfloat16


def split_dot(x, m):
    hi = x.astype(BF16)
    lo = (x - hi.astype(F32)).astype(BF16)
    return jnp.dot(hi, m, preferred_element_type=F32) + jnp.dot(lo, m, preferred_element_type=F32)


def dot_split(m, x):
    hi = x.astype(BF16)
    lo = (x - hi.astype(F32)).astype(BF16)
    return jnp.dot(m, hi, preferred_element_type=F32) + jnp.dot(m, lo, preferred_element_type=F32)


def kernel(
    n, p_ref, o_ref, nrm_ref,
    pv, fv, wv, tmp, c1, c2, ea, eb, sbuf, nbuf, rmat, tmat, lmat, umat,
    in_send, in_recv, halo_send, halo_recv, c_send, c_recv, s_send, s_recv, n_send, n_recv,
    out_send, out_recv, local_sem,
):
    planes, ny, nz = p_ref.shape
    rows = ny // GROUP
    R = rows + 2 * HY
    own = planes * GROUP
    co = own // 2
    total = own + 2 * HX
    cells = float(n * planes * ny * nz)
    me = lax.axis_index("gx")
    member = lax.rem(me, GROUP)
    base = me - member
    right = lax.rem(me + GROUP, n)
    left = lax.rem(me + n - GROUP, n)

    barrier = pltpu.get_barrier_semaphore()

    def greet(k, _):
        pl.semaphore_signal(barrier, inc=1, device_id={"gx": lax.rem(me + k, n)})
        return 0

    lax.fori_loop(1, n, greet, 0)
    pl.semaphore_wait(barrier, n - 1)

    def pieces(t):
        first = t * rows
        return (
            (first, PAD + HY, rows),
            (lax.rem(first + ny - HY, ny), PAD, HY),
            (lax.rem(first + rows, ny), PAD + HY + rows, HY),
        )

    def in_copy(step, piece, start, at, size):
        src = p_ref.at[:, pl.ds(pl.multiple_of(start, 8), size), :]
        dst = pv.at[pl.ds(HX + planes * member, planes), pl.ds(at, size), :]
        if step == 0:
            return pltpu.make_async_copy(src, dst, local_sem.at[piece])
        return pltpu.make_async_remote_copy(
            src, dst, in_send.at[step, piece], in_recv.at[step, piece],
            device_id={"gx": base + lax.rem(member + step, GROUP)},
        )

    sends = []
    for step in (1, 2, 3, 0):
        t = lax.rem(member + step, GROUP)
        for piece, (start, at, size) in enumerate(pieces(t)):
            copy = in_copy(step, piece, start, at, size)
            copy.start()
            sends.append(copy)

    zeros = jnp.zeros((PAD, nz), F32)
    for ref in (pv, fv, wv):
        def clear(i, _, ref=ref):
            ref[i, 0:PAD, :] = zeros
            ref[i, PAD + R : 2 * PAD + R, :] = zeros
            return 0
        lax.fori_loop(0, total, clear, 0)

    def pairs(shape, fine):
        idx = lax.broadcasted_iota(jnp.int32, shape, fine)
        other = lax.broadcasted_iota(jnp.int32, shape, 1 - fine)
        return jnp.where(idx // 2 == other, 1.0, 0.0).astype(BF16)

    rmat[...] = pairs(rmat.shape, 0)
    tmat[...] = pairs(tmat.shape, 1)
    lmat[...] = pairs(lmat.shape, 1)
    umat[...] = pairs(umat.shape, 0)

    for copy in sends:
        copy.wait()

    batch = ((own - 2, 2), (own - 4, 2), (own - 5, 1))
    halos = []
    for b, (at, size) in enumerate(batch):
        halos.append(pltpu.make_async_remote_copy(
            pv.at[pl.ds(HX + at, size), pl.ds(PAD, R), :],
            pv.at[pl.ds(HX + at - own, size), pl.ds(PAD, R), :],
            halo_send.at[0, b], halo_recv.at[0, b], device_id={"gx": right}))
        low = own - at - size
        halos.append(pltpu.make_async_remote_copy(
            pv.at[pl.ds(HX + low, size), pl.ds(PAD, R), :],
            pv.at[pl.ds(HX + own + low, size), pl.ds(PAD, R), :],
            halo_send.at[1, b], halo_recv.at[1, b], device_id={"gx": left}))
    for copy in halos:
        copy.start()
    for copy in halos:
        copy.wait()

    chunks = R // CH

    def at_row(k):
        return pl.multiple_of(PAD + k * CH, 8)

    def window(ref, i, r0):
        return ref[i, pl.ds(pl.multiple_of(r0 - 8, 8), CH + 16), :]

    def up(w):
        return pltpu.roll(w, CH + 15, 0)[8 : 8 + CH]

    def down(w):
        return pltpu.roll(w, 1, 0)[8 : 8 + CH]

    def zp(x):
        return pltpu.roll(x, nz - 1, 1)

    def zm(x):
        return pltpu.roll(x, 1, 1)

    def beside(ref, i, r0):
        w = window(ref, i, r0)
        c = w[8 : 8 + CH]
        s = ref[i - 1, pl.ds(r0, CH), :] + ref[i + 1, pl.ds(r0, CH), :]
        return c, s + (up(w) + down(w)) + (zp(c) + zm(c))

    def own_rows(r0, x):
        row = lax.broadcasted_iota(jnp.int32, (CH, nz), 0) + r0
        return jnp.where((row >= PAD + HY) & (row < PAD + HY + rows), x, 0.0)

    def fold(x):
        t = x[0:8]
        for k in range(1, CH // 8):
            t = t + x[8 * k : 8 * k + 8]
        u = t[:, 0:128]
        for k in range(1, nz // 128):
            u = u + t[:, 128 * k : 128 * k + 128]
        return u

    def over(lo, hi, body, acc=0):
        def plane(i, acc):
            def chunk(k, acc):
                return body(i, at_row(k), acc)
            return lax.fori_loop(0, chunks, chunk, acc)
        return lax.fori_loop(lo, hi, plane, acc)

    acc0 = jnp.zeros((8, 128), F32)

    def source(i, r0):
        w = window(pv, i, r0)
        u = window(pv, i + 1, r0)
        l = window(pv, i - 1, r0)
        c = w[8 : 8 + CH]
        cu, cd = up(w), down(w)
        c2x = 2.0 * c
        xx = u[8 : 8 + CH] + l[8 : 8 + CH] - c2x
        yy = cu + cd - c2x
        zz = zp(c) + zm(c) - c2x
        d = u - l
        xy = up(d) - down(d)
        dc = d[8 : 8 + CH]
        xz = zp(dc) - zm(dc)
        g = cu - cd
        yz = zp(g) - zm(g)
        return xx * yy + (xx + yy) * zz - 0.0625 * (xy * xy + xz * xz + yz * yz)

    def source_body(i, r0, acc):
        s = source(i, r0)
        fv[i, pl.ds(r0, CH), :] = -s
        return acc

    def source_own(i, r0, acc):
        s = source(i, r0)
        fv[i, pl.ds(r0, CH), :] = -s
        return acc + fold(own_rows(r0, s))

    acc = over(HX, HX + own, source_own, acc0)

    def share(buf, send, recv, k):
        return pltpu.make_async_remote_copy(
            buf.at[0], buf.at[k], send.at[k], recv.at[k],
            device_id={"gx": lax.rem(me + k, n)})

    def share_start(buf, send, recv):
        def go(k, _):
            share(buf, send, recv, k).start()
            return 0
        lax.fori_loop(1, n, go, 0)

    def share_wait(buf, send, recv):
        def go(k, _):
            share(buf, send, recv, k).wait()
            return 0
        lax.fori_loop(1, n, go, 0)
        return lax.fori_loop(1, n, lambda k, t: t + buf[k], buf[0])

    sbuf[0] = acc
    over(1, HX, source_body)
    over(HX + own, total - 1, source_body)
    share_start(sbuf, s_send, s_recv)

    def restrict_into(c, lo, hi, residual):
        def plane(j, _):
            i = HX + 2 * (j - 5)
            def chunk(k, _):
                r0 = at_row(k)
                tmp[pl.ds(pl.multiple_of(k * CH, 8), CH), :] = residual(i, r0) + residual(i + 1, r0)
                return 0
            lax.fori_loop(0, chunks, chunk, 0)
            half = dot_split(lmat[...], tmp[...])
            c[j] = split_dot(half, rmat[...]) * 0.125
            return 0
        lax.fori_loop(lo, hi, plane, 0)

    def residual_first(i, r0):
        c, s = beside(fv, i, r0)
        return c - A * (6.0 * c - s)

    restrict_into(c1, 4, 6 + co, residual_first)

    def coarse_trade(c, to_right, at_right, to_left, at_left, slot):
        copies = (
            pltpu.make_async_remote_copy(
                c.at[pl.ds(to_right, 4)], c.at[pl.ds(at_right, 4)],
                c_send.at[slot, 0], c_recv.at[slot, 0], device_id={"gx": right}),
            pltpu.make_async_remote_copy(
                c.at[pl.ds(to_left, 4)], c.at[pl.ds(at_left, 4)],
                c_send.at[slot, 1], c_recv.at[slot, 1], device_id={"gx": left}),
        )
        for copy in copies:
            copy.start()
        for copy in copies:
            copy.wait()

    coarse_trade(c1, co, 0, 6, 6 + co, 0)
    mean = jnp.sum(share_wait(sbuf, s_send, s_recv)) / cells

    cr, cc = c1.shape[1:]

    def coarse_solve(c, lo, hi, shift):
        def first(j, _):
            f = (c[j] + shift) * 4.0
            c[j] = f
            ea[j] = A * f
            return 0
        lax.fori_loop(lo, hi, first, 0)
        src, dst = ea, eb
        for sweep in range(1, 4):
            def again(j, _, src=src, dst=dst):
                v = src[j]
                s = src[j - 1] + src[j + 1]
                s = s + pltpu.roll(v, 1, 0) + pltpu.roll(v, cr - 1, 0)
                s = s + pltpu.roll(v, 1, 1) + pltpu.roll(v, cc - 1, 1)
                dst[j] = 0.2 * v + A * (c[j] + s)
                return 0
            lax.fori_loop(lo + sweep, hi - sweep, again, 0)
            src, dst = dst, src
        return src

    def prolonged(e, j):
        x = e[j]
        return dot_split(umat[...], split_dot(x, tmat[...]))

    e1 = coarse_solve(c1, 0, 10 + co, mean)

    def add_first(j, _):
        tmp[...] = prolonged(e1, j)
        i = HX + 2 * (j - 5)
        def chunk(k, _):
            r0 = at_row(k)
            x = tmp[pl.ds(pl.multiple_of(k * CH, 8), CH), :]
            for q in range(2):
                f = fv[i + q, pl.ds(r0, CH), :] + mean
                fv[i + q, pl.ds(r0, CH), :] = f
                pv[i + q, pl.ds(r0, CH), :] = A * f + x
            return 0
        lax.fori_loop(0, chunks, chunk, 0)
        return 0

    lax.fori_loop(3, 7 + co, add_first, 0)

    def relax_body(src, dst):
        def body(i, r0, acc):
            c, s = beside(src, i, r0)
            dst[i, pl.ds(r0, CH), :] = 0.2 * c + A * (fv[i, pl.ds(r0, CH), :] + s)
            return acc
        return body

    over(2, total - 2, relax_body(pv, wv))

    def relax_norm(i, r0, acc):
        c, s = beside(wv, i, r0)
        r = fv[i, pl.ds(r0, CH), :] - (6.0 * c - s)
        pv[i, pl.ds(r0, CH), :] = c + A * r
        return acc + fold(own_rows(r0, r * r))

    over(3, HX, relax_body(wv, pv))
    norm1 = over(HX, HX + own, relax_norm, acc0)
    over(HX + own, total - 3, relax_body(wv, pv))

    def residual_second(i, r0):
        c, s = beside(pv, i, r0)
        return fv[i, pl.ds(r0, CH), :] - (6.0 * c - s)

    restrict_into(c2, 5, 5 + co, residual_second)
    coarse_trade(c2, 1 + co, 1, 5, 5 + co, 1)
    e2 = coarse_solve(c2, 1, 9 + co, 0.0)

    def add_second(j, _):
        tmp[...] = prolonged(e2, j)
        i = HX + 2 * (j - 5)
        def chunk(k, _):
            r0 = at_row(k)
            x = tmp[pl.ds(pl.multiple_of(k * CH, 8), CH), :]
            for q in range(2):
                pv[i + q, pl.ds(r0, CH), :] = pv[i + q, pl.ds(r0, CH), :] + x
            return 0
        lax.fori_loop(0, chunks, chunk, 0)
        return 0

    lax.fori_loop(4, 6 + co, add_second, 0)
    over(4, total - 4, relax_body(pv, wv))

    def out_copy(step):
        t = lax.rem(member + step, GROUP)
        src = wv.at[pl.ds(HX + planes * t, planes), pl.ds(PAD + HY, rows), :]
        dst = o_ref.at[:, pl.ds(pl.multiple_of(member * rows, 8), rows), :]
        if step == 0:
            return pltpu.make_async_copy(src, dst, local_sem.at[3])
        return pltpu.make_async_remote_copy(
            src, dst, out_send.at[step], out_recv.at[step], device_id={"gx": base + t})

    outs = [out_copy(step) for step in (1, 2, 3, 0)]
    for copy in outs:
        copy.start()

    def norm_body(i, r0, acc):
        c, s = beside(wv, i, r0)
        r = fv[i, pl.ds(r0, CH), :] - (6.0 * c - s)
        return acc + fold(own_rows(r0, r * r))

    norm2 = over(HX, HX + own, norm_body, acc0)
    nbuf[0, 0:8, :] = norm1
    nbuf[0, 8:16, :] = norm2
    share_start(nbuf, n_send, n_recv)
    sums = share_wait(nbuf, n_send, n_recv)
    nrm_ref[0:8, :] = jnp.sqrt(jnp.full((8, 128), jnp.sum(sums[0:8]) / cells, F32))
    nrm_ref[8:16, :] = jnp.sqrt(jnp.full((8, 128), jnp.sum(sums[8:16]) / cells, F32))
    for copy in outs:
        copy.wait()


def on_device(n, potential):
    planes, ny, nz = potential.shape
    R = ny // GROUP + 2 * HY
    total = planes * GROUP + 2 * HX
    coarse = planes * GROUP // 2 + 10
    fine = pltpu.VMEM((total, R + 2 * PAD, nz), F32)
    small = pltpu.VMEM((coarse, R // 2, nz // 2), F32)
    dma = pltpu.SemaphoreType.DMA
    field, norms = pl.pallas_call(
        functools.partial(kernel, n),
        out_shape=(
            jax.ShapeDtypeStruct(potential.shape, F32),
            jax.ShapeDtypeStruct((16, 128), F32),
        ),
        in_specs=[pl.BlockSpec(memory_space=pl.ANY)],
        out_specs=(pl.BlockSpec(memory_space=pl.ANY), pl.BlockSpec(memory_space=pltpu.VMEM)),
        scratch_shapes=[
            fine, fine, fine, pltpu.VMEM((R, nz), F32), small, small, small, small,
            pltpu.VMEM((n, 8, 128), F32), pltpu.VMEM((n, 16, 128), F32),
            pltpu.VMEM((nz, nz // 2), BF16), pltpu.VMEM((nz // 2, nz), BF16),
            pltpu.VMEM((R // 2, R), BF16), pltpu.VMEM((R, R // 2), BF16),
            dma((4, 3)), dma((4, 3)), dma((2, 3)), dma((2, 3)), dma((2, 2)), dma((2, 2)),
            dma((n,)), dma((n,)), dma((n,)), dma((n,)), dma((4,)), dma((4,)), dma((4,)),
        ],
        compiler_params=pltpu.CompilerParams(
            collective_id=0, has_side_effects=True, vmem_limit_bytes=60 << 20),
        name="vcycles",
    )(potential)
    return field, jnp.stack([norms[0, 0], norms[8, 0]])


def solution(mesh):
    n = mesh.shape["gx"]
    return jax.shard_map(
        functools.partial(on_device, n),
        mesh=mesh,
        in_specs=P(("runs", "gx"), None, None),
        out_specs=(P(("runs", "gx"), None, None), P("runs")),
        check_vma=False,
    )
```

time: 576 us -> 276 us (0.48)
  Pallas kernels: 0 us -> 268 us
  local copies, waits for them, and re-layouts: 180 us -> 4.28 us
  waiting for transfers between devices: 132 us -> 0 us
  starting transfers between devices: 104 us -> 0 us
  other arithmetic: 79.7 us -> 1.78 us
  blocking collectives: 69.9 us -> 0 us
    pallas_call x0 -> x1, Pallas kernels: none -> 268 us  [on_device(): pl.pallas_call(functools.partial(kernel, n), out_shape=(jax.ShapeDtypeStr...]
    reduce_sum x2 -> x0, local copies, waits for them, and re-layouts: 137 us -> none  [restrict(): return jnp.mean(blocks, axis=(1, 3, 5))]
    ppermute x30 -> x0, waiting for transfers between devices: 132 us -> none  [the longest x15 94.7 us: with_halo(): lax.ppermute(tail, axis, [(i, (i + 1) % count) for i in range(count)])]
    ppermute x30 -> x0, starting transfers between devices: 104 us -> none  [the longest x15 92.5 us: with_halo(): lax.ppermute(tail, axis, [(i, (i + 1) % count) for i in range(count)])]
    psum x2 -> x0, blocking collectives: 69.9 us -> none  [the longest x1 37.3 us: report_norm(): squares = lax.psum(jnp.sum(residue * residue), 'gx')]
    reduce_sum x7 -> x0, other arithmetic: 64.5 us -> none  [the longest x4 47.4 us: restrict(): return jnp.mean(blocks, axis=(1, 3, 5))]
    slice x69 -> x1, local copies, waits for them, and re-layouts: 27.2 us -> 1.2 us  [on_device(): return (field, jnp.stack([norms[0, 0], norms[8, 0]]))]
    broadcast_in_dim x12 -> x0, local copies, waits for them, and re-layouts: 12.4 us -> none  [prolong(): return jnp.repeat(jnp.repeat(jnp.repeat(field, 2, 0), 2, 1), 2, 2)]
  transfers between devices with their start and end apart: 30 -> 0, of which waited for: 25 -> 0; matrix products, arithmetic and copies ran while one was open for 24% -> 0% of each run, Pallas kernels for 0% -> 0%
where the time goes in v1:
time: 276 us; the launch traced here: 274 us
  Pallas kernels  268 us (97%)
  local copies, waits for them, and re-layouts  4.28 us (2%)
    pallas_call x1, Pallas kernels, on_device(): pl.pallas_call(functools.partial(kernel, n), out_shape=(jax.ShapeDtypeStr...  268 us

profile of v1, /device:TPU:0, one launch (start us, length us, event | category | flops | bytes accessed | tf_op | source)
XLA Modules:
  0.0 274.4 jit_solution(172664560371854836)
XLA Ops:
  0.6 267.7 %vcycles.1 = (f32[2,512,512]{2,1,0:T(8,128)}, f32[16,128]{1,0:T(8,128)}) custom-call(f32[2,512,512]{2,1,0:T(8,128)} %p_ref.1), custom_call_target="tpu_custom_call" | custom-call | tf_op jit(solution)/shard_map/vcycles/pallas_call | solution.py:384
  268.4 1.2 fusion
  269.6 1.8 pad_maximum_fusion
  271.4 3.1 %copy.4 = f32[2,512,512]{2,1,0:T(8,128)} copy(f32[2,512,512]{2,1,0:T(8,128)} %get-tuple-element.10) | data formatting | bytes 4194304

commit v2 on v1

v2 whole, which is shorter than its diff:
```python
import functools

import jax
import jax.numpy as jnp
from jax import lax
from jax.experimental import pallas as pl
from jax.experimental.pallas import tpu as pltpu
from jax.sharding import PartitionSpec as P

HY = 24
PAD = 8
A = 0.8 / 6.0
F32 = jnp.float32
BF16 = jnp.bfloat16


def split_dot(x, m):
    hi = x.astype(BF16)
    lo = (x - hi.astype(F32)).astype(BF16)
    return jnp.dot(hi, m, preferred_element_type=F32) + jnp.dot(lo, m, preferred_element_type=F32)


def dot_split(m, x):
    hi = x.astype(BF16)
    lo = (x - hi.astype(F32)).astype(BF16)
    return jnp.dot(m, hi, preferred_element_type=F32) + jnp.dot(m, lo, preferred_element_type=F32)


def kernel(
    n, p_ref, o_ref, nrm_ref,
    pv, fv, wv, tmp, cf, ea, eb, sbuf, nbuf, rmat, tmat, lmat, umat,
    in_send, in_recv, halo_send, halo_recv, s_send, s_recv, n_send, n_recv,
    out_send, out_recv, local_sem,
):
    planes, ny, nz = p_ref.shape
    rows = ny // n
    R = rows + 2 * HY
    blocks = R // 8
    nx = planes * n
    half = nx // 2
    cells = float(nx * ny * nz)
    chips = n // 2
    me = lax.axis_index("gx")

    def ring_of(d):
        chip = d // 2
        odd = chip % 2
        pos = (1 - odd) * (chip // 2) + odd * (chips - 1 - chip // 2)
        return 2 * pos + d % 2

    def device_at(r):
        pos = r // 2
        back = pos // (chips // 2)
        chip = (1 - back) * (2 * pos) + back * (2 * (chips - 1 - pos) + 1)
        return 2 * chip + r % 2

    def partner(k):
        t = 0
        bit = 1
        while bit < n:
            t = t + (((me // bit) % 2 + (k // bit) % 2) % 2) * bit
            bit *= 2
        return t

    here = ring_of(me)

    barrier = pltpu.get_barrier_semaphore()

    def greet(k, _):
        pl.semaphore_signal(barrier, inc=1, device_id={"gx": lax.rem(me + k, n)})
        return 0

    lax.fori_loop(1, n, greet, 0)
    pl.semaphore_wait(barrier, n - 1)

    def in_copy(k):
        t = partner(k)
        src = p_ref.at[:, pl.ds(pl.multiple_of(ring_of(t) * rows, 8), rows), :]
        dst = pv.at[pl.ds(planes * me, planes), pl.ds(PAD + HY, rows), :]
        if k == 0:
            return pltpu.make_async_copy(src, dst, local_sem.at[0])
        return pltpu.make_async_remote_copy(
            src, dst, in_send.at[k], in_recv.at[k], device_id={"gx": t})

    ins = [in_copy(k) for k in range(n)]
    for k in range(n - 1, -1, -1):
        ins[k].start()

    zeros = jnp.zeros((PAD, nz), F32)

    def clear(i, _):
        for ref in (pv, fv, wv):
            ref[i, 0:PAD, :] = zeros
            ref[i, PAD + R : 2 * PAD + R, :] = zeros
        return 0

    lax.fori_loop(0, nx, clear, 0)

    def pairs(shape, fine):
        idx = lax.broadcasted_iota(jnp.int32, shape, fine)
        other = lax.broadcasted_iota(jnp.int32, shape, 1 - fine)
        return jnp.where(idx // 2 == other, 1.0, 0.0).astype(BF16)

    rmat[...] = pairs(rmat.shape, 0)
    tmat[...] = pairs(tmat.shape, 1)
    lmat[...] = pairs(lmat.shape, 1)
    umat[...] = pairs(umat.shape, 0)

    def halo_copies(b, start):
        copies = []
        at = PAD + HY
        for h in range((HY + rows - 1) // rows):
            size = min(rows, HY - h * rows)
            span = pl.ds(start, half)
            copies.append(pltpu.make_async_remote_copy(
                pv.at[span, pl.ds(at + rows - size, size), :],
                pv.at[span, pl.ds(at - h * rows - size, size), :],
                halo_send.at[b, 0, h], halo_recv.at[b, 0, h],
                device_id={"gx": device_at((here + 1 + h) % n)}))
            copies.append(pltpu.make_async_remote_copy(
                pv.at[span, pl.ds(at, size), :],
                pv.at[span, pl.ds(at + rows + h * rows, size), :],
                halo_send.at[b, 1, h], halo_recv.at[b, 1, h],
                device_id={"gx": device_at((here + n - 1 - h) % n)}))
        return copies

    mine = me // (n // 2)
    far = (1 - mine) * half
    near = mine * half
    for k in range(n - 1, n // 2 - 1, -1):
        ins[k].wait()
    halos = halo_copies(0, far)
    for copy in halos:
        copy.start()
    for k in range(n // 2 - 1, -1, -1):
        ins[k].wait()
    more = halo_copies(1, near)
    for copy in more:
        copy.start()
    for copy in halos + more:
        copy.wait()

    def spans(lo, hi):
        out = []
        while lo < hi:
            size = min(2, hi - lo)
            out.append((PAD + 8 * lo, 8 * size))
            lo += size
        return out

    def before(i):
        return lax.rem(i + nx - 1, nx)

    def after(i):
        return lax.rem(i + 1, nx)

    def zp(x):
        return pltpu.roll(x, nz - 1, 1)

    def zm(x):
        return pltpu.roll(x, 1, 1)

    def beside(ref, i, r, size):
        c = ref[i, r : r + size, :]
        s = ref[before(i), r : r + size, :] + ref[after(i), r : r + size, :]
        y = ref[i, r - 1 : r - 1 + size, :] + ref[i, r + 1 : r + 1 + size, :]
        return c, s + y + (zp(c) + zm(c))

    def fold(x):
        t = x[0:8]
        for k in range(1, x.shape[0] // 8):
            t = t + x[8 * k : 8 * k + 8]
        u = t[:, 0:128]
        for k in range(1, nz // 128):
            u = u + t[:, 128 * k : 128 * k + 128]
        return u

    def over(lo, hi, body, acc=0, start=0, count=nx):
        def plane(i, acc):
            for r, size in spans(lo, hi):
                acc = body(i, r, size, acc)
            return acc
        return lax.fori_loop(start, start + count, plane, acc)

    own = (HY // 8, blocks - HY // 8)
    acc0 = jnp.zeros((8, 128), F32)

    def source(i, r, size):
        lower, upper = before(i), after(i)
        def at(k, q):
            return pv[k, r + q : r + q + size, :]
        c, cu, cd = at(i, 0), at(i, 1), at(i, -1)
        u, l = at(upper, 0), at(lower, 0)
        c2x = 2.0 * c
        xx = u + l - c2x
        yy = cu + cd - c2x
        zz = zp(c) + zm(c) - c2x
        xy = (at(upper, 1) - at(lower, 1)) - (at(upper, -1) - at(lower, -1))
        d = u - l
        xz = zp(d) - zm(d)
        g = cu - cd
        yz = zp(g) - zm(g)
        return xx * yy + (xx + yy) * zz - 0.0625 * (xy * xy + xz * xz + yz * yz)

    def source_plane(i, acc):
        for lo, hi in ((0, own[0]), own, (own[1], blocks)):
            for r, size in spans(lo, hi):
                s = source(i, r, size)
                fv[i, r : r + size, :] = -s
                if (lo, hi) == own:
                    acc = acc + fold(s)
        return acc

    sbuf[0] = lax.fori_loop(0, nx, source_plane, acc0)

    def share(buf, send, recv, k):
        return pltpu.make_async_remote_copy(
            buf.at[0], buf.at[k], send.at[k], recv.at[k],
            device_id={"gx": lax.rem(me + k, n)})

    def share_start(buf, send, recv):
        def go(k, _):
            share(buf, send, recv, k).start()
            return 0
        lax.fori_loop(1, n, go, 0)

    def share_wait(buf, send, recv):
        def go(k, _):
            share(buf, send, recv, k).wait()
            return 0
        lax.fori_loop(1, n, go, 0)
        return lax.fori_loop(1, n, lambda k, t: t + buf[k], buf[0])

    share_start(sbuf, s_send, s_recv)

    def restrict(lo, hi, residual):
        def plane(j, _):
            for r, size in spans(lo, hi):
                tmp[r - PAD : r - PAD + size, :] = residual(2 * j, r, size) + residual(2 * j + 1, r, size)
            cf[j] = split_dot(dot_split(lmat[...], tmp[...]), rmat[...]) * 0.125
            return 0
        lax.fori_loop(0, half, plane, 0)

    def residual_first(i, r, size):
        c, s = beside(fv, i, r, size)
        return c - A * (6.0 * c - s)

    restrict(0, blocks, residual_first)
    mean = jnp.sum(share_wait(sbuf, s_send, s_recv)) / cells

    cr, cc = cf.shape[1:]

    def coarse_solve(shift):
        def first(j, _):
            f = (cf[j] + shift) * 4.0
            cf[j] = f
            ea[j] = A * f
            return 0
        lax.fori_loop(0, half, first, 0)
        src, dst = ea, eb
        for sweep in range(3):
            def again(j, _, src=src, dst=dst):
                v = src[j]
                s = src[lax.rem(j + half - 1, half)] + src[lax.rem(j + 1, half)]
                s = s + pltpu.roll(v, 1, 0) + pltpu.roll(v, cr - 1, 0)
                s = s + pltpu.roll(v, 1, 1) + pltpu.roll(v, cc - 1, 1)
                dst[j] = 0.2 * v + A * (cf[j] + s)
                return 0
            lax.fori_loop(0, half, again, 0)
            src, dst = dst, src
        return src

    def prolong(e, lo, hi, add):
        def plane(j, _):
            tmp[...] = dot_split(umat[...], split_dot(e[j], tmat[...]))
            for r, size in spans(lo, hi):
                x = tmp[r - PAD : r - PAD + size, :]
                for q in range(2):
                    add(2 * j + q, r, size, x)
            return 0
        lax.fori_loop(0, half, plane, 0)

    def add_first(i, r, size, x):
        f = fv[i, r : r + size, :] + mean
        fv[i, r : r + size, :] = f
        pv[i, r : r + size, :] = A * f + x

    def add_second(i, r, size, x):
        pv[i, r : r + size, :] = pv[i, r : r + size, :] + x

    def relax(i, r, size, acc):
        c, s = beside(pv, i, r, size)
        wv[i, r : r + size, :] = 0.2 * c + A * (fv[i, r : r + size, :] + s)
        return acc

    def residual_of(ref, i, r, size):
        c, s = beside(ref, i, r, size)
        return c, fv[i, r : r + size, :] - (6.0 * c - s)

    def relax_norm(i, acc):
        for lo, hi in ((1, own[0]), own, (own[1], blocks - 1)):
            for r, size in spans(lo, hi):
                c, res = residual_of(wv, i, r, size)
                pv[i, r : r + size, :] = c + A * res
                if (lo, hi) == own:
                    acc = acc + fold(res * res)
        return acc

    prolong(coarse_solve(mean), 1, blocks - 1, add_first)
    over(1, blocks - 1, relax)
    nbuf[0, 0:8, :] = lax.fori_loop(0, nx, relax_norm, acc0)

    restrict(2, blocks - 2, lambda i, r, size: residual_of(pv, i, r, size)[1])
    prolong(coarse_solve(0.0), 2, blocks - 2, add_second)

    def out_copy(k):
        t = partner(k)
        src = wv.at[pl.ds(planes * t, planes), pl.ds(PAD + HY, rows), :]
        dst = o_ref.at[:, pl.ds(pl.multiple_of(here * rows, 8), rows), :]
        if k == 0:
            return pltpu.make_async_copy(src, dst, local_sem.at[1])
        return pltpu.make_async_remote_copy(
            src, dst, out_send.at[k], out_recv.at[k], device_id={"gx": t})

    outs = [out_copy(k) for k in range(n)]
    over(2, blocks - 2, relax, start=far, count=half)
    for k in range(n - 1, n // 2 - 1, -1):
        outs[k].start()
    over(2, blocks - 2, relax, start=near, count=half)
    for k in range(n // 2 - 1, -1, -1):
        outs[k].start()

    def norm_body(i, r, size, acc):
        res = residual_of(wv, i, r, size)[1]
        return acc + fold(res * res)

    nbuf[0, 8:16, :] = over(*own, norm_body, acc0)
    share_start(nbuf, n_send, n_recv)
    sums = share_wait(nbuf, n_send, n_recv)
    nrm_ref[0:8, :] = jnp.sqrt(jnp.full((8, 128), jnp.sum(sums[0:8]) / cells, F32))
    nrm_ref[8:16, :] = jnp.sqrt(jnp.full((8, 128), jnp.sum(sums[8:16]) / cells, F32))
    for copy in outs:
        copy.wait()


def on_device(n, potential):
    planes, ny, nz = potential.shape
    R = ny // n + 2 * HY
    nx = planes * n
    cr = (R // 2 + 7) // 8 * 8
    hops = -(-HY // (ny // n))
    fine = pltpu.VMEM((nx, R + 2 * PAD, nz), F32)
    small = pltpu.VMEM((nx // 2, cr, nz // 2), F32)
    dma = pltpu.SemaphoreType.DMA
    field, norms = pl.pallas_call(
        functools.partial(kernel, n),
        out_shape=(
            jax.ShapeDtypeStruct(potential.shape, F32),
            jax.ShapeDtypeStruct((16, 128), F32),
        ),
        in_specs=[pl.BlockSpec(memory_space=pl.ANY)],
        out_specs=(pl.BlockSpec(memory_space=pl.ANY), pl.BlockSpec(memory_space=pltpu.VMEM)),
        scratch_shapes=[
            fine, fine, fine, pltpu.VMEM((R, nz), F32), small, small, small,
            pltpu.VMEM((n, 8, 128), F32), pltpu.VMEM((n, 16, 128), F32),
            pltpu.VMEM((nz, nz // 2), BF16), pltpu.VMEM((nz // 2, nz), BF16),
            pltpu.VMEM((cr, R), BF16), pltpu.VMEM((R, cr), BF16),
            dma((n,)), dma((n,)), dma((2, 2, hops)), dma((2, 2, hops)),
            dma((n,)), dma((n,)), dma((n,)), dma((n,)), dma((n,)), dma((n,)), dma((2,)),
        ],
        compiler_params=pltpu.CompilerParams(
            collective_id=0, has_side_effects=True, vmem_limit_bytes=67043328),
        name="vcycles",
    )(potential)
    return field, jnp.stack([norms[0, 0], norms[8, 0]])


def solution(mesh):
    n = mesh.shape["gx"]
    return jax.shard_map(
        functools.partial(on_device, n),
        mesh=mesh,
        in_specs=P(("runs", "gx"), None, None),
        out_specs=(P(("runs", "gx"), None, None), P("runs")),
        check_vma=False,
    )
```

time: 276 us -> 195 us (0.71)
  Pallas kernels: 268 us -> 188 us
    pallas_call x1, Pallas kernels: 268 us -> 188 us  [on_device(): pl.pallas_call(functools.partial(kernel, n), out_shape=(jax.ShapeDtypeStr...]
where the time goes in v2:
time: 195 us
  Pallas kernels  188 us (96%)
  local copies, waits for them, and re-layouts  4.28 us (2%)
    pallas_call x1, Pallas kernels, on_device(): pl.pallas_call(functools.partial(kernel, n), out_shape=(jax.ShapeDtypeStr...  188 us

profile of v2, /device:TPU:0, one launch (start us, length us, event | category | flops | bytes accessed | tf_op | source)
XLA Modules:
  0.0 194.7 jit_solution(15657667875038155783)
XLA Ops:
  0.6 188.0 %vcycles.1 = (f32[2,512,512]{2,1,0:T(8,128)}, f32[16,128]{1,0:T(8,128)}) custom-call(f32[2,512,512]{2,1,0:T(8,128)} %p_ref.1), custom_call_target="tpu_custom_call" | custom-call | tf_op jit(solution)/shard_map/vcycles/pallas_call | solution.py:355
  188.6 1.2 fusion
  189.8 1.8 pad_maximum_fusion
  191.6 3.1 %copy.4 = f32[2,512,512]{2,1,0:T(8,128)} copy(f32[2,512,512]{2,1,0:T(8,128)} %get-tuple-element.10) | data formatting | bytes 4194304

commit v3 on v2

--- a/solution.py
+++ b/solution.py
@@ -20,15 +20,9 @@
     return jnp.dot(hi, m, preferred_element_type=F32) + jnp.dot(lo, m, preferred_element_type=F32)
 
 
-def dot_split(m, x):
-    hi = x.astype(BF16)
-    lo = (x - hi.astype(F32)).astype(BF16)
-    return jnp.dot(m, hi, preferred_element_type=F32) + jnp.dot(m, lo, preferred_element_type=F32)
-
-
 def kernel(
     n, p_ref, o_ref, nrm_ref,
-    pv, fv, wv, tmp, cf, ea, eb, sbuf, nbuf, rmat, tmat, lmat, umat,
+    pv, fv, wv, tmp, cf, ea, eb, sbuf, nbuf, rmat, tmat,
     in_send, in_recv, halo_send, halo_recv, s_send, s_recv, n_send, n_recv,
     out_send, out_recv, local_sem,
 ):
@@ -83,8 +77,10 @@
             src, dst, in_send.at[k], in_recv.at[k], device_id={"gx": t})
 
     ins = [in_copy(k) for k in range(n)]
-    for k in range(n - 1, -1, -1):
-        ins[k].start()
+    quarter = n // 4
+    for k in range(quarter):
+        for q in (3, 1, 2, 0):
+            ins[q * quarter + k].start()
 
     zeros = jnp.zeros((PAD, nz), F32)
 
@@ -103,15 +99,13 @@
 
     rmat[...] = pairs(rmat.shape, 0)
     tmat[...] = pairs(tmat.shape, 1)
-    lmat[...] = pairs(lmat.shape, 1)
-    umat[...] = pairs(umat.shape, 0)
 
     def halo_copies(b, start):
         copies = []
         at = PAD + HY
         for h in range((HY + rows - 1) // rows):
             size = min(rows, HY - h * rows)
-            span = pl.ds(start, half)
+            span = pl.ds(start, nx // 4)
             copies.append(pltpu.make_async_remote_copy(
                 pv.at[span, pl.ds(at + rows - size, size), :],
                 pv.at[span, pl.ds(at - h * rows - size, size), :],
@@ -127,17 +121,16 @@
     mine = me // (n // 2)
     far = (1 - mine) * half
     near = mine * half
-    for k in range(n - 1, n // 2 - 1, -1):
-        ins[k].wait()
-    halos = halo_copies(0, far)
+    halos = []
+    for b, q in enumerate((1, 0, 3, 2)):
+        for k in range(quarter):
+            ins[q * quarter + k].wait()
+        z = partner(q * quarter) // quarter
+        copies = halo_copies(b, z * (nx // 4))
+        for copy in copies:
+            copy.start()
+        halos += copies
     for copy in halos:
-        copy.start()
-    for k in range(n // 2 - 1, -1, -1):
-        ins[k].wait()
-    more = halo_copies(1, near)
-    for copy in more:
-        copy.start()
-    for copy in halos + more:
         copy.wait()
 
     def spans(lo, hi):
@@ -233,13 +226,32 @@
 
     share_start(sbuf, s_send, s_recv)
 
+    cr, cc = cf.shape[1:]
+    batch = 4
+    lanes = [(256 * k, 128 * k) for k in range(nz // 256)]
+    slabs = range(nz // 128)
+    wide = wv.at[:, PAD : PAD + cr, :]
+
     def restrict(lo, hi, residual):
+        first, last = 4 * lo, 4 * hi
         def plane(j, _):
             for r, size in spans(lo, hi):
-                tmp[r - PAD : r - PAD + size, :] = residual(2 * j, r, size) + residual(2 * j + 1, r, size)
-            cf[j] = split_dot(dot_split(lmat[...], tmp[...]), rmat[...]) * 0.125
+                x = residual(2 * j, r, size) + residual(2 * j + 1, r, size)
+                for q in slabs:
+                    tmp[q, r - PAD : r - PAD + size, :] = x[:, 128 * q : 128 * q + 128]
+            span = last - first
+            for q in slabs:
+                x = tmp[q, pl.ds(2 * first, span, stride=2), :] + tmp[q, pl.ds(2 * first + 1, span, stride=2), :]
+                wide[j, first:last, 128 * q : 128 * q + 128] = x * 0.125
             return 0
         lax.fori_loop(0, half, plane, 0)
+        def lane_pairs(b, _):
+            at = pl.ds(b * batch, batch)
+            for fine, coarse in lanes:
+                x = wide[at, :, fine : fine + 256].reshape(batch * cr, 256)
+                cf[at, :, coarse : coarse + 128] = split_dot(x, rmat[...]).reshape(batch, cr, 128)
+            return 0
+        lax.fori_loop(0, half // batch, lane_pairs, 0)
 
     def residual_first(i, r, size):
         c, s = beside(fv, i, r, size)
@@ -247,8 +259,6 @@
 
     restrict(0, blocks, residual_first)
     mean = jnp.sum(share_wait(sbuf, s_send, s_recv)) / cells
-
-    cr, cc = cf.shape[1:]
 
     def coarse_solve(shift):
         def first(j, _):
@@ -271,10 +281,21 @@
         return src
 
     def prolong(e, lo, hi, add):
+        first, span = 4 * lo, 4 * (hi - lo)
+        def lane_pairs(b, _):
+            at = pl.ds(b * batch, batch)
+            for fine, coarse in lanes:
+                x = e[at, :, coarse : coarse + 128].reshape(batch * cr, 128)
+                wide[at, :, fine : fine + 256] = split_dot(x, tmat[...]).reshape(batch, cr, 256)
+            return 0
+        lax.fori_loop(0, half // batch, lane_pairs, 0)
         def plane(j, _):
-            tmp[...] = dot_split(umat[...], split_dot(e[j], tmat[...]))
+            for q in slabs:
+                x = wide[j, first : first + span, 128 * q : 128 * q + 128]
+                tmp[q, pl.ds(2 * first, span, stride=2), :] = x
+                tmp[q, pl.ds(2 * first + 1, span, stride=2), :] = x
             for r, size in spans(lo, hi):
-                x = tmp[r - PAD : r - PAD + size, :]
+                x = jnp.concatenate([tmp[q, r - PAD : r - PAD + size, :] for q in slabs], axis=1)
                 for q in range(2):
                     add(2 * j + q, r, size, x)
             return 0
@@ -361,11 +382,10 @@
         in_specs=[pl.BlockSpec(memory_space=pl.ANY)],
         out_specs=(pl.BlockSpec(memory_space=pl.ANY), pl.BlockSpec(memory_space=pltpu.VMEM)),
         scratch_shapes=[
-            fine, fine, fine, pltpu.VMEM((R, nz), F32), small, small, small,
+            fine, fine, fine, pltpu.VMEM((nz // 128, R, 128), F32), small, small, small,
             pltpu.VMEM((n, 8, 128), F32), pltpu.VMEM((n, 16, 128), F32),
-            pltpu.VMEM((nz, nz // 2), BF16), pltpu.VMEM((nz // 2, nz), BF16),
-            pltpu.VMEM((cr, R), BF16), pltpu.VMEM((R, cr), BF16),
-            dma((n,)), dma((n,)), dma((2, 2, hops)), dma((2, 2, hops)),
+            pltpu.VMEM((256, 128), BF16), pltpu.VMEM((128, 256), BF16),
+            dma((n,)), dma((n,)), dma((4, 2, hops)), dma((4, 2, hops)),
             dma((n,)), dma((n,)), dma((n,)), dma((n,)), dma((n,)), dma((n,)), dma((2,)),
         ],
         compiler_params=pltpu.CompilerParams(

time: 195 us -> 174 us (0.89)
  Pallas kernels: 188 us -> 167 us
    pallas_call x1, Pallas kernels: 188 us -> 167 us  [on_device(): pl.pallas_call(functools.partial(kernel, n), out_shape=(jax.ShapeDtypeStr...]
where the time goes in v3:
time: 174 us
  Pallas kernels  167 us (96%)
  local copies, waits for them, and re-layouts  4.28 us (2%)
  other arithmetic  1.78 us (1%)
    pallas_call x1, Pallas kernels, on_device(): pl.pallas_call(functools.partial(kernel, n), out_shape=(jax.ShapeDtypeStr...  167 us

profile of v3, /device:TPU:0, one launch (start us, length us, event | category | flops | bytes accessed | tf_op | source)
XLA Modules:
  0.0 174.1 jit_solution(3763822665107140572)
XLA Ops:
  0.6 167.4 %vcycles.1 = (f32[2,512,512]{2,1,0:T(8,128)}, f32[16,128]{1,0:T(8,128)}) custom-call(f32[2,512,512]{2,1,0:T(8,128)} %p_ref.1), custom_call_target="tpu_custom_call" | custom-call | tf_op jit(solution)/shard_map/vcycles/pallas_call | solution.py:376
  168.0 1.2 fusion
  169.2 1.8 %pad_maximum_fusion = f32[2]{0:T(128)} fusion(f32[1]{0:T(128)} %bitcast.1, f32[1]{0:T(128)} %bitcast), kind=kLoop, calls=%fused_computation | loop fusion | flops 2 | bytes 16 | tf_op jit(solution)/shard_map/stack | solution.py:395
  171.0 3.1 %copy.4 = f32[2,512,512]{2,1,0:T(8,128)} copy(f32[2,512,512]{2,1,0:T(8,128)} %get-tuple-element.10) | data formatting | bytes 4194304

commit v4 on v3

--- a/solution.py
+++ b/solution.py
@@ -18,6 +18,14 @@
     hi = x.astype(BF16)
     lo = (x - hi.astype(F32)).astype(BF16)
     return jnp.dot(hi, m, preferred_element_type=F32) + jnp.dot(lo, m, preferred_element_type=F32)
+
+
+def loop(lo, count, body, acc, by):
+    def some(h, acc):
+        for q in range(by):
+            acc = body(lo + by * h + q, acc)
+        return acc
+    return lax.fori_loop(0, count // by, some, acc)
 
 
 def kernel(
@@ -118,9 +126,6 @@
                 device_id={"gx": device_at((here + n - 1 - h) % n)}))
         return copies
 
-    mine = me // (n // 2)
-    far = (1 - mine) * half
-    near = mine * half
     halos = []
     for b, q in enumerate((1, 0, 3, 2)):
         for k in range(quarter):
@@ -173,7 +178,7 @@
             for r, size in spans(lo, hi):
                 acc = body(i, r, size, acc)
             return acc
-        return lax.fori_loop(start, start + count, plane, acc)
+        return loop(start, count, plane, acc, 4)
 
     own = (HY // 8, blocks - HY // 8)
     acc0 = jnp.zeros((8, 128), F32)
@@ -204,7 +209,7 @@
                     acc = acc + fold(s)
         return acc
 
-    sbuf[0] = lax.fori_loop(0, nx, source_plane, acc0)
+    sbuf[0] = loop(0, nx, source_plane, acc0, 2)
 
     def share(buf, send, recv, k):
         return pltpu.make_async_remote_copy(
@@ -227,24 +232,25 @@
     share_start(sbuf, s_send, s_recv)
 
     cr, cc = cf.shape[1:]
-    batch = 4
+    batch = 8
     lanes = [(256 * k, 128 * k) for k in range(nz // 256)]
-    slabs = range(nz // 128)
+    slabs_n = nz // 128
+    slabs = range(slabs_n)
     wide = wv.at[:, PAD : PAD + cr, :]
 
     def restrict(lo, hi, residual):
         first, last = 4 * lo, 4 * hi
-        def plane(j, _):
+        def plane(j, _, z):
             for r, size in spans(lo, hi):
                 x = residual(2 * j, r, size) + residual(2 * j + 1, r, size)
                 for q in slabs:
-                    tmp[q, r - PAD : r - PAD + size, :] = x[:, 128 * q : 128 * q + 128]
+                    tmp[z + q, r - PAD : r - PAD + size, :] = x[:, 128 * q : 128 * q + 128]
             span = last - first
             for q in slabs:
-                x = tmp[q, pl.ds(2 * first, span, stride=2), :] + tmp[q, pl.ds(2 * first + 1, span, stride=2), :]
+                x = tmp[z + q, pl.ds(2 * first, span, stride=2), :] + tmp[z + q, pl.ds(2 * first + 1, span, stride=2), :]
                 wide[j, first:last, 128 * q : 128 * q + 128] = x * 0.125
             return 0
-        lax.fori_loop(0, half, plane, 0)
+        lax.fori_loop(0, half // 2, lambda h, a: plane(2 * h + 1, plane(2 * h, a, 0), slabs_n), 0)
         def lane_pairs(b, _):
             at = pl.ds(b * batch, batch)
             for fine, coarse in lanes:
@@ -266,7 +272,7 @@
             cf[j] = f
             ea[j] = A * f
             return 0
-        lax.fori_loop(0, half, first, 0)
+        loop(0, half, first, 0, 4)
         src, dst = ea, eb
         for sweep in range(3):
             def again(j, _, src=src, dst=dst):
@@ -276,7 +282,7 @@
                 s = s + pltpu.roll(v, 1, 1) + pltpu.roll(v, cc - 1, 1)
                 dst[j] = 0.2 * v + A * (cf[j] + s)
                 return 0
-            lax.fori_loop(0, half, again, 0)
+            loop(0, half, again, 0, 4)
             src, dst = dst, src
         return src
 
@@ -289,17 +295,17 @@
                 wide[at, :, fine : fine + 256] = split_dot(x, tmat[...]).reshape(batch, cr, 256)
             return 0
         lax.fori_loop(0, half // batch, lane_pairs, 0)
-        def plane(j, _):
+        def plane(j, _, z):
             for q in slabs:
                 x = wide[j, first : first + span, 128 * q : 128 * q + 128]
-                tmp[q, pl.ds(2 * first, span, stride=2), :] = x
-                tmp[q, pl.ds(2 * first + 1, span, stride=2), :] = x
+                tmp[z + q, pl.ds(2 * first, span, stride=2), :] = x
+                tmp[z + q, pl.ds(2 * first + 1, span, stride=2), :] = x
             for r, size in spans(lo, hi):
-                x = jnp.concatenate([tmp[q, r - PAD : r - PAD + size, :] for q in slabs], axis=1)
+                x = jnp.concatenate([tmp[z + q, r - PAD : r - PAD + size, :] for q in slabs], axis=1)
                 for q in range(2):
                     add(2 * j + q, r, size, x)
             return 0
-        lax.fori_loop(0, half, plane, 0)
+        lax.fori_loop(0, half // 2, lambda h, a: plane(2 * h + 1, plane(2 * h, a, 0), slabs_n), 0)
 
     def add_first(i, r, size, x):
         f = fv[i, r : r + size, :] + mean
@@ -329,7 +335,7 @@
 
     prolong(coarse_solve(mean), 1, blocks - 1, add_first)
     over(1, blocks - 1, relax)
-    nbuf[0, 0:8, :] = lax.fori_loop(0, nx, relax_norm, acc0)
+    nbuf[0, 0:8, :] = loop(0, nx, relax_norm, acc0, 4)
 
     restrict(2, blocks - 2, lambda i, r, size: residual_of(pv, i, r, size)[1])
     prolong(coarse_solve(0.0), 2, blocks - 2, add_second)
@@ -344,12 +350,11 @@
             src, dst, out_send.at[k], out_recv.at[k], device_id={"gx": t})
 
     outs = [out_copy(k) for k in range(n)]
-    over(2, blocks - 2, relax, start=far, count=half)
-    for k in range(n - 1, n // 2 - 1, -1):
-        outs[k].start()
-    over(2, blocks - 2, relax, start=near, count=half)
-    for k in range(n // 2 - 1, -1, -1):
-        outs[k].start()
+    for q in (3, 2, 1, 0):
+        z = partner(q * quarter) // quarter
+        over(2, blocks - 2, relax, start=z * (nx // 4), count=nx // 4)
+        for k in range(quarter):
+            outs[q * quarter + k].start()
 
     def norm_body(i, r, size, acc):
         res = residual_of(wv, i, r, size)[1]
@@ -382,7 +387,7 @@
         in_specs=[pl.BlockSpec(memory_space=pl.ANY)],
         out_specs=(pl.BlockSpec(memory_space=pl.ANY), pl.BlockSpec(memory_space=pltpu.VMEM)),
         scratch_shapes=[
-            fine, fine, fine, pltpu.VMEM((nz // 128, R, 128), F32), small, small, small,
+            fine, fine, fine, pltpu.VMEM((2 * nz // 128, R, 128), F32), small, small, small,
             pltpu.VMEM((n, 8, 128), F32), pltpu.VMEM((n, 16, 128), F32),
             pltpu.VMEM((256, 128), BF16), pltpu.VMEM((128, 256), BF16),
             dma((n,)), dma((n,)), dma((4, 2, hops)), dma((4, 2, hops)),

time: 174 us -> 162 us (0.931)
  Pallas kernels: 167 us -> 155 us
    pallas_call x1, Pallas kernels: 167 us -> 155 us  [on_device(): pl.pallas_call(functools.partial(kernel, n), out_shape=(jax.ShapeDtypeStr...]
where the time goes in v4:
time: 162 us
  Pallas kernels  155 us (96%)
  local copies, waits for them, and re-layouts  4.28 us (3%)
  other arithmetic  1.78 us (1%)
    pallas_call x1, Pallas kernels, on_device(): pl.pallas_call(functools.partial(kernel, n), out_shape=(jax.ShapeDtypeStr...  155 us

profile of v4, /device:TPU:0, one launch (start us, length us, event | category | flops | bytes accessed | tf_op | source)
XLA Modules:
  0.0 162.1 jit_solution(12792963618378369066)
XLA Ops:
  0.6 155.4 %vcycles.1 = (f32[2,512,512]{2,1,0:T(8,128)}, f32[16,128]{1,0:T(8,128)}) custom-call(f32[2,512,512]{2,1,0:T(8,128)} %p_ref.1), custom_call_target="tpu_custom_call" | custom-call | tf_op jit(solution)/shard_map/vcycles/pallas_call | solution.py:381
  156.0 1.2 fusion
  157.2 1.8 %pad_maximum_fusion = f32[2]{0:T(128)} fusion(f32[1]{0:T(128)} %bitcast.1, f32[1]{0:T(128)} %bitcast), kind=kLoop, calls=%fused_computation | loop fusion | flops 2 | bytes 16 | tf_op jit(solution)/shard_map/stack | solution.py:400
  159.0 3.1 %copy.4 = f32[2,512,512]{2,1,0:T(8,128)} copy(f32[2,512,512]{2,1,0:T(8,128)} %get-tuple-element.10) | data formatting | bytes 4194304
